TPU v7x, 32 devices: a whole 2x2x4 slice. The times are simulated.
32 devices in a mesh: row: 8 (over z, x), col: 4 (over y, core).
Axes of the slice: x: 2, y: 2, z: 4, core: 2. Of those that a mesh axis runs over, the one named last changes fastest.
Arguments:
- features: bfloat16 [32768, 256], P(('col', 'row')), may hold values from -6 to 6
- adjacency: bfloat16 [256, 4, 12, 128, 128], P('row', 'col'), may hold values from 0 to 0.023925781
- block_cols: int32 [256, 4, 12], P('row', 'col'), may hold values from 0 to 63, as said below
- block_live: int32 [256, 4], P('row', 'col'), may hold values from 1 to 12, as said below
- weight: bfloat16 [256, 256], replicated, may hold values from -0.375 to 0.375
- bias: float32 [256], replicated, may hold values from -3 to 3
- upstream: bfloat16 [32768, 256], P(('row', 'col')), may hold values from -6 to 6
Outputs:
- activations: bfloat16 [32768, 256], P(('row', 'col'))
- feature_grad: bfloat16 [32768, 256], P(('col', 'row'))
- weight_grad: float32 [256, 256], replicated
- bias_grad: float32 [256], replicated
Inputs may be any that keep to these rules, and one draw needn't show every extreme that they name: `block_cols`: the live slots of one block row in one column tile name distinct column blocks of that tile. Slots k with k < block_live[i, c] are live; the other slots of block_cols and adjacency are ignored. Some entry equals 12.
All inputs are finite; a program needn't handle non-finite values.
Results may differ from a plain program's by a relative error of at most 0.014.
Values may be sent and summed in bfloat16 or wider, within the bound.
No kernel may reach another device: no remote copies, remote signals or barrier semaphores. Data moves between devices by JAX's collectives and lax.ppermute only.
A program may use at most 256 MiB of HBM per device.

v0:
```python
import jax
import jax.numpy as jnp
from jax import lax
from jax.sharding import PartitionSpec as P


def local(features, adjacency, block_cols, block_live, weight, bias, upstream):
    block_rows = adjacency.shape[0]
    block_slots = adjacency.shape[2]
    block_size = adjacency.shape[3]
    feature_width = features.shape[1]
    tile_blocks = adjacency.reshape(block_rows, block_slots, block_size, block_size)
    column_ids = block_cols.reshape(block_rows, block_slots)
    live_count = block_live.reshape(block_rows)
    live_mask = lax.broadcasted_iota(jnp.int32, (block_rows, block_slots), 1) < live_count[:, None]
    feature_panel = lax.all_gather(features, "row", axis=0, tiled=True)
    panel_blocks = feature_panel.shape[0] // block_size
    picked = feature_panel.reshape(panel_blocks, block_size, feature_width)[column_ids]
    picked = jnp.where(live_mask[:, :, None, None], picked, jnp.zeros((), jnp.bfloat16))
    partial_value = jnp.einsum(
        "ikab,ikbf->iaf", tile_blocks, picked, preferred_element_type=jnp.float32
    )
    partial_value = partial_value.reshape(block_rows * block_size, feature_width)
    aggregated = lax.psum_scatter(partial_value, "col", scatter_dimension=0, tiled=True).astype(
        jnp.bfloat16
    )
    preact = jnp.dot(aggregated, weight, preferred_element_type=jnp.float32) + bias
    sigmoid_pre = jax.nn.sigmoid(preact)
    outputs_here = (preact * sigmoid_pre).astype(jnp.bfloat16)
    derivative = sigmoid_pre * (1.0 + preact * (1.0 - sigmoid_pre))
    grad_pre = (upstream.astype(jnp.float32) * derivative).astype(jnp.bfloat16)
    weight_part = jnp.einsum("nf,ng->fg", aggregated, grad_pre, preferred_element_type=jnp.float32)
    bias_part = jnp.sum(grad_pre.astype(jnp.float32), axis=0)
    grad_agg = jnp.einsum("ng,fg->nf", grad_pre, weight, preferred_element_type=jnp.float32).astype(
        jnp.bfloat16
    )
    weight_grad, bias_grad = lax.psum((weight_part, bias_part), ("row", "col"))
    tile_grad = lax.all_gather(grad_agg, "col", axis=0, tiled=True)
    contrib = jnp.einsum(
        "ikab,iaf->ikbf",
        tile_blocks,
        tile_grad.reshape(block_rows, block_size, feature_width),
        preferred_element_type=jnp.float32,
    )
    contrib = contrib.reshape(block_rows * block_slots, block_size, feature_width)
    target_blocks = jnp.where(live_mask, column_ids, panel_blocks).reshape(-1)
    panel_sum = jnp.zeros((panel_blocks, block_size, feature_width), jnp.float32)
    panel_sum = panel_sum.at[target_blocks].add(contrib, mode="drop")
    panel_sum = panel_sum.reshape(panel_blocks * block_size, feature_width)
    feature_grad = lax.psum_scatter(
        panel_sum.astype(jnp.bfloat16), "row", scatter_dimension=0, tiled=True
    )
    return (outputs_here, feature_grad, weight_grad, bias_grad)


def solution(mesh):
    placed = (
        P(("col", "row"), None),
        P("row", "col", None, None, None),
        P("row", "col", None),
        P("row", "col"),
        P(),
        P(),
        P(("row", "col"), None),
    )
    return jax.shard_map(
        local,
        mesh=mesh,
        in_specs=placed,
        out_specs=(P(("row", "col"), None), P(("col", "row"), None), P(), P()),
        check_vma=False,
    )
```

profile of v0, /device:TPU:0, one launch (start us, length us, event | category | flops | bytes accessed | tf_op | source)
XLA Modules:
  0.0 477.4 jit_solution(3709703805803400464)
XLA Ops:
  7.2 0.0 copy-start
  7.2 0.0 all-gather.3.cloned.1.call-start
  7.2 0.7 all-gather.3.cloned.1.call-update
  7.9 0.0 reduce-scatter.3.cloned.1.call-start
  8.0 0.7 compare_select_fusion
  8.7 0.1 copy.12
  8.8 0.1 reshape.129
  8.9 0.7 iota_compare_fusion
  9.6 76.1 %all-gather.3.cloned.1.call-done = bf16[8192,256]{1,0:T(8,128)(2,1)} async-done(((bf16[1024,256]{1,0:T(8,128)(2,1)}), bf16[8192,256]{1,0:T(8,128)(2,1)}) %all-gather.3.cloned.1.call-update) | async-done | bytes 4194320 | tf_op jit(solution)/shard_map/all_gather | solution.py:16
  85.7 15.1 %gather_fusion = bf16[384,128,256]{2,1,0:T(8,128)(2,1)} fusion(bf16[64,128,256]{2,1,0:T(8,128)(2,1)} %bitcast.35, s32[1024]{0:T(1024)S(1)} %pad_clamp_fusion), kind=kCustom, calls=%fused_computation | custom fusion | bytes 50333184 | tf_op jit(solution)/shard_map/gather | solution.py:18
  100.8 0.0 copy-start.3
  100.8 0.0 copy-start.4
  100.8 16.1 %fusion = f32[32,256,128,1]{1,2,3,0:T(8,128)} fusion(bf16[32,12,128,256]{3,2,1,0:T(8,128)(2,1)} %bitcast.36, pred[32,12]{1,0:T(8,128)(4,1)S(1)} %iota_compare_fusion, bf16[32,1,12,128,128]{4,3,2,1,0:T(8,128)(2,1)} %param.8), kind=kOutput, calls=%fused_computation.2 | convolution fusion | flops 3233808384 | bytes 41943424 | tf_op jit(solution)/shard_map/ikab,ikbf->iaf/dot_general | solution.py:20
  116.9 0.0 copy-start.2
  116.9 0.0 reduce-scatter.3.cloned.1.call-update
  116.9 0.0 all-gather.5.cloned.1.call-start
  116.9 43.2 %reduce-scatter.3.cloned.1.call-done = f32[1024,256]{1,0:T(8,128)} async-done(((f32[4096,256]{1,0:T(8,128)}), f32[1024,256]{1,0:T(8,128)}) %reduce-scatter.3.cloned.1.call-update) | async-done | bytes 1048592 | tf_op jit(solution)/shard_map/reduce_scatter | solution.py:24
  160.2 0.0 copy-done
  160.2 0.0 copy-done.3
  160.2 0.0 copy-done.4
  160.2 2.7 convert_reduce_fusion
  162.9 1.1 convolution_convert_fusion
  164.0 0.0 all-gather.5.cloned.1.call-update
  164.0 0.0 all-reduce.2.cloned.1.call-start
  164.1 0.1 lt.53
  164.2 0.0 copy-done.2
  164.2 0.1 copy.13
  164.3 0.1 reshape.124
  164.4 2.3 fusion.7
  166.7 0.0 all-reduce.2.cloned.1.call-update
  166.7 0.0 reduce-scatter.5.cloned.1.call-start
  166.8 20.0 %all-gather.5.cloned.1.call-done = bf16[4096,256]{1,0:T(8,128)(2,1)} async-done(((bf16[1024,256]{1,0:T(8,128)(2,1)}), bf16[4096,256]{1,0:T(8,128)(2,1)}) %all-gather.5.cloned.1.call-update) | async-done | bytes 2097168 | tf_op jit(solution)/shard_map/all_gather | solution.py:38
  186.7 22.5 %fusion.3 = f32[32,256,12,128]{3,1,2,0:T(8,128)} fusion(bf16[32,128,256,1]{2,1,3,0:T(8,128)(2,1)} %bitcast.39, bf16[32,1,12,128,128]{4,3,2,1,0:T(8,128)(2,1)} %param.8), kind=kOutput, calls=%fused_computation.5 | convolution fusion | flops 3221225472 | bytes 65011712 | tf_op jit(solution)/shard_map/ikab,iaf->ikbf/dot_general | solution.py:39
  209.3 48.9 %copy.15 = f32[384,128,256]{2,1,0:T(8,128)} copy(f32[384,128,256]{1,2,0:T(8,128)} %bitcast.34) | data formatting | bytes 100663296 | tf_op jit(solution)/shard_map/reshape | solution.py:45
  258.2 4.2 broadcast_in_dim.23
  262.4 0.0 copy-start.1
  262.4 109.8 %scatter_fusion = f32[64,128,256]{2,1,0:T(8,128)} fusion(f32[64,128,256]{2,1,0:T(8,128)} %broadcast_in_dim.23, s32[384]{0:T(512)S(1)} %fusion.10, f32[384,128,256]{2,1,0:T(8,128)} %copy.15), kind=kCustom, calls=%fused_computation.1 | custom fusion | flops 12582912 | bytes 150996480 | tf_op jit(solution)/shard_map/scatter-add | solution.py:48
  372.2 5.9 %convert_element_type.29 = bf16[64,128,256]{2,1,0:T(8,128)(2,1)} convert(f32[64,128,256]{2,1,0:T(8,128)} %scatter_fusion) | non-fusion elementwise | flops 2097152 | bytes 12582912 | tf_op jit(solution)/shard_map/convert_element_type | solution.py:51
  378.1 0.0 reduce-scatter.5.cloned.1.call-update
  378.1 43.6 %psum.15 = f32[256]{0:T(256)} all-reduce(f32[256]{0:T(256)S(1)} %get-tuple-element.4), channel_id=1, replica_groups=mesh['row'=8,'col'=4] {'row','col'}, use_global_device_ids=true, to_apply=%region_5.6 | all-reduce | flops 256 | bytes 2048 | tf_op jit(solution)/shard_map/psum | solution.py:37
  421.8 0.0 all-reduce.2.cloned.1.call-done
  421.8 47.4 %reduce-scatter.5.cloned.1.call-done = bf16[1024,256]{1,0:T(8,128)(2,1)} async-done(((bf16[8192,256]{1,0:T(8,128)(2,1)}), bf16[1024,256]{1,0:T(8,128)(2,1)}) %reduce-scatter.5.cloned.1.call-update) | async-done | bytes 524304 | tf_op jit(solution)/shard_map/reduce_scatter | solution.py:50
  469.2 1.7 copy.22
  470.8 0.0 copy-done.1
  (2 shorter events, 0.0 us)
Async XLA Ops:
  7.2 153.0 %copy-start = (bf16[256,256]{1,0:T(8,128)(2,1)S(1)}, bf16[256,256]{1,0:T(8,128)(2,1)}, u32[]{:S(2)}) copy-start(bf16[256,256]{1,0:T(8,128)(2,1)} %param.11) | copy-start | bytes 393220
  7.2 78.5 %all-gather.3.cloned.1.call-start = ((), (), s32[]{:S(2)}) async-start(), calls=%async_computation.2 | async-start | bytes 4718592 | tf_op jit(solution)/shard_map/all_gather | solution.py:16
  7.9 152.3 %reduce-scatter.3.cloned.1.call-start = ((), (), s32[]{:S(2)}) async-start(), calls=%async_computation.3 | async-start | bytes 5242880 | tf_op jit(solution)/shard_map/reduce_scatter | solution.py:24
  100.8 59.4 %copy-start.3 = (bf16[1024,256]{1,0:T(8,128)(2,1)S(1)}, bf16[1024,256]{1,0:T(8,128)(2,1)}, u32[]{:S(2)}) copy-start(bf16[1024,256]{1,0:T(8,128)(2,1)} %param.13) | copy-start | bytes 1572868
  100.8 59.4 %copy-start.4 = (f32[256]{0:T(256)S(1)}, f32[256]{0:T(256)}, u32[]{:S(2)}) copy-start(f32[256]{0:T(256)} %param.12) | copy-start | bytes 3076
  116.9 47.3 %copy-start.2 = (s32[32,1,12]{0,1,2:T(1,128)S(1)}, s32[32,1,12]{0,1,2:T(1,128)}, u32[]{:S(2)}) copy-start(s32[32,1,12]{0,1,2:T(1,128)} %param.9) | copy-start | bytes 4612
  116.9 69.9 %all-gather.5.cloned.1.call-start = ((), (), s32[]{:S(2)}) async-start(), calls=%async_computation.4 | async-start | bytes 2621440 | tf_op jit(solution)/shard_map/all_gather | solution.py:38
  164.0 257.8 %all-reduce.2.cloned.1.call-start = ((), (), s32[]{:S(2)}) async-start(), calls=%async_computation.6 | async-start | bytes 524288 | tf_op jit(solution)/shard_map/psum | solution.py:37
  166.7 302.4 %reduce-scatter.5.cloned.1.call-start = ((), (), s32[]{:S(2)}) async-start(), calls=%async_computation.5 | async-start | bytes 4718592 | tf_op jit(solution)/shard_map/reduce_scatter | solution.py:50
  262.4 208.4 %copy-start.1 = (bf16[256,256]{1,0:T(8,128)(2,1)S(1)}, bf16[256,256]{1,0:T(8,128)(2,1)}, u32[]{:S(2)}) copy-start(bf16[256,256]{1,0:T(8,128)(2,1)} %param.11) | copy-start | bytes 393220
Sparse Core Ops, SparseCore 0:
  10.1 75.4 all-gather.2
  117.0 43.1 reduce-scatter.2
  164.2 22.5 all-gather.4
  192.7 126.5 all-reduce.1
  378.3 90.8 reduce-scatter.4
where the time goes:
time: 479 us; the launch traced here: 477 us
  waiting for transfers between devices  187 us (39%)
  other arithmetic  117 us (24%)
  local copies, waits for them, and re-layouts  70.4 us (15%)
  matrix products  44.7 us (9%)
  blocking collectives  43.6 us (9%)
  between operations  13.8 us (3%)
    scatter-add x1, other arithmetic, local(): panel_sum = panel_sum.at[target_blocks].add(contrib, mode='drop')  110 us
    all_gather x1, waiting for transfers between devices, local(): feature_panel = lax.all_gather(features, 'row', axis=0, tiled=True)  76.1 us
    reshape x1, local copies, waits for them, and re-layouts, local(): contrib.reshape(block_rows * block_slots, block_size, feature_width)  48.9 us
    reduce_scatter x1, waiting for transfers between devices, local(): lax.psum_scatter(panel_sum.astype(jnp.bfloat16), 'row', scatter_dimension...  47.4 us
    psum x1, blocking collectives, local(): weight_grad, bias_grad = lax.psum((weight_part, bias_part), ('row', 'col'))  43.6 us
    reduce_scatter x1, waiting for transfers between devices, local(): lax.psum_scatter(partial_value, 'col', scatter_dimension=0, tiled=True)  43.2 us
    dot_general x1, matrix products, local(): jnp.einsum('ikab,iaf->ikbf', tile_blocks, tile_grad.reshape(block_rows, b...  22.5 us
    all_gather x1, waiting for transfers between devices, local(): tile_grad = lax.all_gather(grad_agg, 'col', axis=0, tiled=True)  20 us
  transfers between devices with their start and end apart: 5, of which 4 were waited for; matrix products, arithmetic and copies ran while one was open for 41% of the time, Pallas kernels for 0%

commit v1 on v0

--- a/solution.py
+++ b/solution.py
@@ -34,7 +34,7 @@
     grad_agg = jnp.einsum("ng,fg->nf", grad_pre, weight, preferred_element_type=jnp.float32).astype(
         jnp.bfloat16
     )
-    weight_grad, bias_grad = lax.psum((weight_part, bias_part), ("row", "col"))
+    weight_grad, bias_grad = lax.psum(lax.psum((weight_part, bias_part), "col"), "row")
     tile_grad = lax.all_gather(grad_agg, "col", axis=0, tiled=True)
     contrib = jnp.einsum(
         "ikab,iaf->ikbf",

time: 479 us -> 513 us (1.071)
  waiting for transfers between devices: 187 us -> 235 us
  blocking collectives: 43.6 us -> 30.7 us
    psum x1 -> x2, waiting for transfers between devices: 0.01 us -> 30.8 us  [the longest x1 30.8 us: local(): lax.psum((weight_part, bias_part), 'col')]
    psum x1 -> x2, blocking collectives: 43.6 us -> 30.7 us  [the longest x1 23.6 us: local(): lax.psum(lax.psum((weight_part, bias_part), 'col'), 'row')]
    reduce_scatter x1, waiting for transfers between devices: 47.4 us -> 59.8 us  [local(): lax.psum_scatter(panel_sum.astype(jnp.bfloat16), 'row', scatter_dimension...]
  transfers between devices with their start and end apart: 5 -> 6, of which waited for: 4 -> 5; matrix products, arithmetic and copies ran while one was open for 41% -> 38% of each run, Pallas kernels for 0% -> 0%
where the time goes in v1:
time: 513 us; the launch traced here: 512 us
  waiting for transfers between devices  235 us (46%)
  other arithmetic  117 us (23%)
  local copies, waits for them, and re-layouts  70.4 us (14%)
  matrix products  44.7 us (9%)
  blocking collectives  30.7 us (6%)
  between operations  14.2 us (3%)
    scatter-add x1, other arithmetic, local(): panel_sum = panel_sum.at[target_blocks].add(contrib, mode='drop')  109 us
    all_gather x1, waiting for transfers between devices, local(): feature_panel = lax.all_gather(features, 'row', axis=0, tiled=True)  76.1 us
    reduce_scatter x1, waiting for transfers between devices, local(): lax.psum_scatter(panel_sum.astype(jnp.bfloat16), 'row', scatter_dimension...  59.8 us
    reshape x1, local copies, waits for them, and re-layouts, local(): contrib.reshape(block_rows * block_slots, block_size, feature_width)  48.9 us
    reduce_scatter x1, waiting for transfers between devices, local(): lax.psum_scatter(partial_value, 'col', scatter_dimension=0, tiled=True)  43.2 us
    psum x1, waiting for transfers between devices, local(): lax.psum((weight_part, bias_part), 'col')  30.8 us
    all_gather x1, waiting for transfers between devices, local(): tile_grad = lax.all_gather(grad_agg, 'col', axis=0, tiled=True)  24.5 us
    psum x1, blocking collectives, local(): lax.psum(lax.psum((weight_part, bias_part), 'col'), 'row')  23.6 us
  transfers between devices with their start and end apart: 6, of which 5 were waited for; matrix products, arithmetic and copies ran while one was open for 38% of the time, Pallas kernels for 0%

profile of v1, /device:TPU:0, one launch (start us, length us, event | category | flops | bytes accessed | tf_op | source)
XLA Modules:
  0.0 511.9 jit_solution(1806104329781706127)
XLA Ops:
  7.2 0.0 copy-start
  7.2 0.0 all-gather.3.cloned.1.call-start
  7.2 0.7 all-gather.3.cloned.1.call-update
  7.9 0.0 reduce-scatter.3.cloned.1.call-start
  8.0 0.7 compare_select_fusion
  8.7 0.1 copy.12
  8.8 0.1 reshape.129
  8.9 0.7 iota_compare_fusion
  9.6 76.1 %all-gather.3.cloned.1.call-done = bf16[8192,256]{1,0:T(8,128)(2,1)} async-done(((bf16[1024,256]{1,0:T(8,128)(2,1)}), bf16[8192,256]{1,0:T(8,128)(2,1)}) %all-gather.3.cloned.1.call-update) | async-done | bytes 4194320 | tf_op jit(solution)/shard_map/all_gather | solution.py:16
  85.7 15.1 %gather_fusion = bf16[384,128,256]{2,1,0:T(8,128)(2,1)} fusion(bf16[64,128,256]{2,1,0:T(8,128)(2,1)} %bitcast.35, s32[1024]{0:T(1024)S(1)} %pad_clamp_fusion), kind=kCustom, calls=%fused_computation | custom fusion | bytes 50333184 | tf_op jit(solution)/shard_map/gather | solution.py:18
  100.8 0.0 copy-start.3
  100.8 0.0 copy-start.4
  100.8 16.1 %fusion = f32[32,256,128,1]{1,2,3,0:T(8,128)} fusion(bf16[32,12,128,256]{3,2,1,0:T(8,128)(2,1)} %bitcast.36, pred[32,12]{1,0:T(8,128)(4,1)S(1)} %iota_compare_fusion, bf16[32,1,12,128,128]{4,3,2,1,0:T(8,128)(2,1)} %param.8), kind=kOutput, calls=%fused_computation.2 | convolution fusion | flops 3233808384 | bytes 41943424 | tf_op jit(solution)/shard_map/ikab,ikbf->iaf/dot_general | solution.py:20
  116.9 0.0 copy-start.2
  116.9 0.0 reduce-scatter.3.cloned.1.call-update
  116.9 0.0 all-reduce.3.cloned.1.call-start
  116.9 43.2 %reduce-scatter.3.cloned.1.call-done = f32[1024,256]{1,0:T(8,128)} async-done(((f32[4096,256]{1,0:T(8,128)}), f32[1024,256]{1,0:T(8,128)}) %reduce-scatter.3.cloned.1.call-update) | async-done | bytes 1048592 | tf_op jit(solution)/shard_map/reduce_scatter | solution.py:24
  160.2 0.0 copy-done
  160.2 0.0 copy-done.3
  160.2 0.0 copy-done.4
  160.2 2.7 convert_reduce_fusion
  162.9 2.3 fusion.7
  165.1 0.0 all-reduce.3.cloned.1.call-update
  165.2 0.0 all-gather.5.cloned.1.call-start
  165.2 1.1 convolution_convert_fusion
  166.3 0.0 all-gather.5.cloned.1.call-update
  166.4 0.0 all-reduce.5.cloned.1.call-start
  166.4 0.1 lt.53
  166.5 0.0 copy-done.2
  166.5 0.1 copy.13
  166.6 0.1 reshape.124
  166.7 30.8 %all-reduce.3.cloned.1.call-done = f32[256,256]{1,0:T(8,128)} async-done(((f32[256,256]{1,0:T(8,128)}), f32[256,256]{1,0:T(8,128)}) %all-reduce.3.cloned.1.call-update) | async-done | bytes 262160 | tf_op jit(solution)/shard_map/psum | solution.py:37
  197.6 0.0 all-reduce.5.cloned.1.call-update
  197.6 0.0 reduce-scatter.5.cloned.1.call-start
  197.7 24.5 %all-gather.5.cloned.1.call-done = bf16[4096,256]{1,0:T(8,128)(2,1)} async-done(((bf16[1024,256]{1,0:T(8,128)(2,1)}), bf16[4096,256]{1,0:T(8,128)(2,1)}) %all-gather.5.cloned.1.call-update) | async-done | bytes 2097168 | tf_op jit(solution)/shard_map/all_gather | solution.py:38
  222.2 22.5 %fusion.3 = f32[32,256,12,128]{3,1,2,0:T(8,128)} fusion(bf16[32,128,256,1]{2,1,3,0:T(8,128)(2,1)} %bitcast.39, bf16[32,1,12,128,128]{4,3,2,1,0:T(8,128)(2,1)} %param.8), kind=kOutput, calls=%fused_computation.5 | convolution fusion | flops 3221225472 | bytes 65011712 | tf_op jit(solution)/shard_map/ikab,iaf->ikbf/dot_general | solution.py:39
  244.7 48.9 %copy.15 = f32[384,128,256]{2,1,0:T(8,128)} copy(f32[384,128,256]{1,2,0:T(8,128)} %bitcast.34) | data formatting | bytes 100663296 | tf_op jit(solution)/shard_map/reshape | solution.py:45
  293.5 4.2 broadcast_in_dim.23
  297.8 0.0 copy-start.1
  297.8 109.2 %scatter_fusion = f32[64,128,256]{2,1,0:T(8,128)} fusion(f32[64,128,256]{2,1,0:T(8,128)} %broadcast_in_dim.23, s32[384]{0:T(512)S(1)} %fusion.10, f32[384,128,256]{2,1,0:T(8,128)} %copy.15), kind=kCustom, calls=%fused_computation.1 | custom fusion | flops 12582912 | bytes 150996480 | tf_op jit(solution)/shard_map/scatter-add | solution.py:48
  407.0 5.9 %convert_element_type.29 = bf16[64,128,256]{2,1,0:T(8,128)(2,1)} convert(f32[64,128,256]{2,1,0:T(8,128)} %scatter_fusion) | non-fusion elementwise | flops 2097152 | bytes 12582912 | tf_op jit(solution)/shard_map/convert_element_type | solution.py:51
  412.9 0.0 reduce-scatter.5.cloned.1.call-update
  412.9 7.0 %psum.30 = f32[256]{0:T(256)S(1)} all-reduce(f32[256]{0:T(256)S(1)} %get-tuple-element.4), channel_id=1, replica_groups=mesh['row'=8,'col'=4] {'col'}, use_global_device_ids=true, to_apply=%region_6.7 | all-reduce | flops 256 | bytes 2048 | tf_op jit(solution)/shard_map/psum | solution.py:37
  420.0 23.6 %psum.31 = f32[256]{0:T(256)} all-reduce(f32[256]{0:T(256)S(1)} %psum.30), channel_id=1, replica_groups=mesh['row'=8,'col'=4] {'row'}, use_global_device_ids=true, to_apply=%region_7.8 | all-reduce | flops 256 | bytes 2048 | tf_op jit(solution)/shard_map/psum | solution.py:37
  443.6 0.0 all-reduce.5.cloned.1.call-done
  443.6 59.8 %reduce-scatter.5.cloned.1.call-done = bf16[1024,256]{1,0:T(8,128)(2,1)} async-done(((bf16[8192,256]{1,0:T(8,128)(2,1)}), bf16[1024,256]{1,0:T(8,128)(2,1)}) %reduce-scatter.5.cloned.1.call-update) | async-done | bytes 524304 | tf_op jit(solution)/shard_map/reduce_scatter | solution.py:50
  503.4 1.7 copy.23
  505.1 0.0 copy-done.1
  (2 shorter events, 0.0 us)
Async XLA Ops:
  7.2 153.0 %copy-start = (bf16[256,256]{1,0:T(8,128)(2,1)S(1)}, bf16[256,256]{1,0:T(8,128)(2,1)}, u32[]{:S(2)}) copy-start(bf16[256,256]{1,0:T(8,128)(2,1)} %param.11) | copy-start | bytes 393220
  7.2 78.5 %all-gather.3.cloned.1.call-start = ((), (), s32[]{:S(2)}) async-start(), calls=%async_computation.2 | async-start | bytes 4718592 | tf_op jit(solution)/shard_map/all_gather | solution.py:16
  7.9 152.2 %reduce-scatter.3.cloned.1.call-start = ((), (), s32[]{:S(2)}) async-start(), calls=%async_computation.3 | async-start | bytes 5242880 | tf_op jit(solution)/shard_map/reduce_scatter | solution.py:24
  100.8 59.4 %copy-start.3 = (bf16[1024,256]{1,0:T(8,128)(2,1)S(1)}, bf16[1024,256]{1,0:T(8,128)(2,1)}, u32[]{:S(2)}) copy-start(bf16[1024,256]{1,0:T(8,128)(2,1)} %param.13) | copy-start | bytes 1572868
  100.8 59.4 %copy-start.4 = (f32[256]{0:T(256)S(1)}, f32[256]{0:T(256)}, u32[]{:S(2)}) copy-start(f32[256]{0:T(256)} %param.12) | copy-start | bytes 3076
  116.9 49.7 %copy-start.2 = (s32[32,1,12]{0,1,2:T(1,128)S(1)}, s32[32,1,12]{0,1,2:T(1,128)}, u32[]{:S(2)}) copy-start(s32[32,1,12]{0,1,2:T(1,128)} %param.9) | copy-start | bytes 4612
  116.9 80.7 %all-reduce.3.cloned.1.call-start = ((), (), s32[]{:S(2)}) async-start(), calls=%async_computation.6 | async-start | bytes 524288 | tf_op jit(solution)/shard_map/psum | solution.py:37
  165.2 57.0 %all-gather.5.cloned.1.call-start = ((), (), s32[]{:S(2)}) async-start(), calls=%async_computation.4 | async-start | bytes 2621440 | tf_op jit(solution)/shard_map/all_gather | solution.py:38
  166.4 277.3 %all-reduce.5.cloned.1.call-start = ((), (), s32[]{:S(2)}) async-start(), calls=%async_computation.7 | async-start | bytes 524288 | tf_op jit(solution)/shard_map/psum | solution.py:37
  197.6 305.8 %reduce-scatter.5.cloned.1.call-start = ((), (), s32[]{:S(2)}) async-start(), calls=%async_computation.5 | async-start | bytes 4718592 | tf_op jit(solution)/shard_map/reduce_scatter | solution.py:50
  297.8 207.3 %copy-start.1 = (bf16[256,256]{1,0:T(8,128)(2,1)S(1)}, bf16[256,256]{1,0:T(8,128)(2,1)}, u32[]{:S(2)}) copy-start(bf16[256,256]{1,0:T(8,128)(2,1)} %param.11) | copy-start | bytes 393220
Sparse Core Ops, SparseCore 0:
  10.1 75.4 all-gather.2
  117.0 43.1 reduce-scatter.2
  165.3 32.2 all-reduce.2
  199.6 22.5 all-gather.4
  225.4 71.0 all-reduce.4
  413.1 90.3 reduce-scatter.4
